TPU v7x, 256 devices: a whole 4x4x8 slice. The times are simulated.
256 devices in a mesh: region: 8 (over x, core), sub: 32 (over y, z).
Axes of the slice: x: 4, y: 4, z: 8, core: 2. Of those that a mesh axis runs over, the one named last changes fastest.
Arguments:
- multipliers: float32 [256, 3, 3, 256], P(('region', 'sub')), may hold values from -6 to 6
- direction: float32 [256, 3, 3, 256], P(('region', 'sub')), may hold values from -12 to 12
- residual: float32 [256, 3, 3, 256], P(('region', 'sub')), may hold values from -12 to 12
- reaction: float32 [256, 16, 256], P(('region', 'sub')), may hold values from 0.1 to 2
- viscosity: float32 [256, 16, 256], P(('region', 'sub')), may hold values from 0.5 to 5
- primal_index: int32 [256, 96], P(('region', 'sub')), may hold values from 17 to 2286, as said below
- region_inverse: float32 [8, 3072, 3072], P('region', 'sub'), as said below
- coarse_map: float32 [256, 96, 384], P(('region', 'sub')), may hold values from -0.4375 to 0.4375
- global_inverse: float32 [384, 384], replicated, as said below
Outputs:
- new_multipliers: float32 [256, 3, 3, 256], P(('region', 'sub'))
- new_residual: float32 [256, 3, 3, 256], P(('region', 'sub'))
- velocity: float32 [256, 3, 16, 256], P(('region', 'sub'))
- pressure: float32 [256, 16, 256], P(('region', 'sub'))
Inputs may be any that keep to these rules, and one draw needn't show every extreme that they name: `primal_index`: each row holds 96 different positions, each in the interior of a face (neither face index 0 nor 16 - 1); every row contains the first such position and the last one. `region_inverse`: each region's matrix is symmetric positive definite. `global_inverse`: symmetric positive definite.
All inputs are finite; a program needn't handle non-finite values.
Results may differ from a plain program's by a relative error of at most 0.0001.
Values sent between devices are 32-bit elements; how exact they have to be, the bound alone decides.
A program may use at most 64 MiB of HBM per device.

v0:
```python
import jax
import jax.numpy as jnp
from jax import lax
from jax.sharding import PartitionSpec as P

DOM_Z = 4
LEVELS = 3
SWEEPS = 1
COARSE_SWEEPS = 8
VCYCLES = 2
damping = 0.8


def shifted_2(x, axis, by):
    count = lax.axis_size(axis)
    return lax.ppermute(x, axis, [(i, (i + by) % count) for i in range(count)])


def operate(field, react, weight, cells):
    width = field.shape[-1]
    padded = jnp.pad(field, ((0, 0), (1, 1), (cells, cells)))
    middle = padded[:, 1:-1]
    position = lax.broadcasted_iota(jnp.int32, (1, 1, width), 2) % cells
    above = jnp.where(position < cells - 1, middle[:, :, cells + 1 : cells + 1 + width], 0.0)
    beneath = jnp.where(position > 0, middle[:, :, cells - 1 : cells - 1 + width], 0.0)
    beside = padded[:, 2:, cells : cells + width] + padded[:, :-2, cells : cells + width]
    beside = beside + middle[:, :, 2 * cells :] + middle[:, :, :width]
    beside = beside + above + beneath
    return react * field + weight * (6.0 * field - beside)


def restrict(array, cells):
    lead = array.shape[:-2]
    depth = array.shape[-2]
    half = cells // 2
    blocks = array.reshape(lead + (depth // 2, 2, half, 2, half, 2)).mean(axis=(-5, -3, -1))
    return blocks.reshape(lead + (depth // 2, half * half))


def prolong(array, cells):
    lead = array.shape[:-2]
    depth = array.shape[-2]
    cubic = array.reshape(lead + (depth, cells, cells))
    grown = jnp.repeat(jnp.repeat(jnp.repeat(cubic, 2, axis=-3), 2, axis=-2), 2, axis=-1)
    return grown.reshape(lead + (2 * depth, 4 * cells * cells))


def relax(field, source, react, weight, cells, count):
    diagonal = react + 6.0 * weight
    for _ in range(count):
        field = field + damping * (source - operate(field, react, weight, cells)) / diagonal
    return field


def vcycle(field, source, reacts, cells, level):
    weight = 0.25**level
    if level == LEVELS - 1:
        return relax(field, source, reacts[level], weight, cells, COARSE_SWEEPS)
    field = relax(field, source, reacts[level], weight, cells, SWEEPS)
    remain = restrict(source - operate(field, reacts[level], weight, cells), cells)
    coarse = vcycle(jnp.zeros_like(remain), remain, reacts, cells // 2, level + 1)
    field = field + prolong(coarse, cells // 2)
    return relax(field, source, reacts[level], weight, cells, SWEEPS)


def local_solve(source, react, cells):
    reacts = [react]
    size_now = cells
    for _ in range(LEVELS - 1):
        reacts.append(restrict(reacts[-1], size_now))
        size_now = size_now // 2
    field = jnp.zeros_like(source)
    for _ in range(VCYCLES):
        field = vcycle(field, source, reacts, cells, 0)
    return field


def face_cells(picked, cells):
    face = cells * cells
    block = picked // (3 * face)
    component = picked // face % 3
    spot = picked % face
    first = spot // cells
    second = spot % cells
    upper = cells - 1
    place = jnp.where(
        block == 0,
        upper * face + spot,
        jnp.where(
            block == 1, first * face + upper * cells + second, first * face + second * cells + upper
        ),
    )
    return component * (cells * face) + place


def body(
    multipliers,
    direction,
    residual,
    reaction,
    viscosity,
    primal_index,
    region_inverse,
    coarse_map,
    global_inverse,
):
    highest = lax.Precision.HIGHEST
    react = reaction[0]
    cells = react.shape[0]
    face = react.shape[1]
    upper_end = cells - 1
    active = direction[0]
    below_x = shifted_2(active[0], "region", 1)
    below_y = shifted_2(active[1], "sub", DOM_Z)
    below_z = shifted_2(active[2], "sub", 1)
    source = jnp.zeros((3, cells, face), jnp.float32)
    source = source.at[:, upper_end, :].add(active[0])
    source = source.at[:, :, face - cells :].add(active[1].reshape(3, cells, cells))
    source = source.at[:, :, upper_end::cells].add(active[2].reshape(3, cells, cells))
    source = source.at[:, 0, :].add(-below_x)
    source = source.at[:, :, :cells].add(-below_y.reshape(3, cells, cells))
    source = source.at[:, :, 0::cells].add(-below_z.reshape(3, cells, cells))
    picked = primal_index[0]
    primal = jnp.take(active.reshape(-1), picked)
    rows = region_inverse[0]
    mapping = coarse_map[0]
    share = jnp.dot(primal, mapping, precision=highest)
    total = lax.psum(share, ("region", "sub"))
    region_part = jnp.dot(
        rows, lax.all_gather(primal, "sub", axis=0, tiled=True), precision=highest
    )
    top = jnp.dot(global_inverse, total, precision=highest)
    lifted = region_part + jnp.dot(mapping, top, precision=highest)
    base = local_solve(source, react, cells)
    spots = face_cells(picked, cells)
    velocity = base.reshape(-1).at[spots].add(lifted).reshape(3, cells, face)
    upper_x = velocity[:, upper_end, :]
    upper_y = velocity[:, :, face - cells :].reshape(3, face)
    upper_z = velocity[:, :, upper_end::cells].reshape(3, face)
    lower_x = velocity[:, 0, :]
    lower_y = velocity[:, :, :cells].reshape(3, face)
    lower_z = velocity[:, :, 0::cells].reshape(3, face)
    squares = jnp.sum(residual[0] * residual[0])
    after_x = shifted_2(lower_x, "region", -1)
    after_y = shifted_2(lower_y, "sub", -DOM_Z)
    after_z = shifted_2(lower_z, "sub", -1)
    jump = jnp.stack([upper_x - after_x, upper_y - after_y, upper_z - after_z])
    curvature, squares_all = lax.psum((jnp.sum(active * jump), squares), ("region", "sub"))
    step_x = jnp.concatenate([velocity[0, 1:], after_x[0][None]], axis=0) - velocity[0]
    step_y = (
        jnp.concatenate([velocity[1][:, cells:], after_y[1].reshape(cells, cells)], axis=1)
        - velocity[1]
    )
    position = lax.broadcasted_iota(jnp.int32, (1, face), 1) % cells
    edge_values = jnp.repeat(after_z[2].reshape(cells, cells), cells, axis=1)
    shifted = jnp.pad(velocity[2][:, 1:], ((0, 0), (0, 1)))
    step_z = jnp.where(position == cells - 1, edge_values, shifted) - velocity[2]
    pressure = -viscosity[0] * (step_x + step_y + step_z)
    alpha = squares_all / curvature
    new_multipliers = (multipliers[0] + alpha * active)[None]
    new_residual = (residual[0] - alpha * jump)[None]
    return (new_multipliers, new_residual, velocity[None], pressure[None])


def solution(mesh):
    in_specs = (
        P(("region", "sub"), None, None, None),
        P(("region", "sub"), None, None, None),
        P(("region", "sub"), None, None, None),
        P(("region", "sub"), None, None),
        P(("region", "sub"), None, None),
        P(("region", "sub"), None),
        P("region", "sub", None),
        P(("region", "sub"), None, None),
        P(),
    )
    out_specs = (
        P(("region", "sub"), None, None, None),
        P(("region", "sub"), None, None, None),
        P(("region", "sub"), None, None, None),
        P(("region", "sub"), None, None),
    )
    return jax.shard_map(body, mesh=mesh, in_specs=in_specs, out_specs=out_specs, check_vma=False)
```

profile of v0, /device:TPU:1, one launch (start us, length us, event | category | flops | bytes accessed | tf_op | source)
XLA Modules:
  0.0 369.7 jit_solution(10086883032054162801)
XLA Ops:
  1.5 2.6 collective-permute-start
  4.1 6.9 %collective-permute-start.1 = (f32[3,256]{1,0:T(4,128)S(1)}, f32[3,256]{1,0:T(4,128)S(1)}, u32[]{:S(2)}, u32[]{:S(2)}) collective-permute-start(f32[3,256]{1,0:T(4,128)S(1)} %bitcast.181), channel_id=1, source_target_pairs={{0,4},{1,5},{2,6},{3,7},{4,8},{5,9},{6,10},{7,11},{8,12},{9,13},{1... | collective-permute-start | bytes 9224 | tf_op jit(solution)/shard_map/ppermute | solution.py:16
  13.2 1.7 reshape_squeeze.17
  16.5 1.1 gather_fusion
  19.1 114.8 %all-reduce.28 = f32[3072]{0:T(1024)S(1)} all-reduce(f32[3072]{0:T(1024)S(1)} %fusion.269), channel_id=1, replica_groups=mesh['region'=8,'sub'=32] {'sub'}, use_global_device_ids=true, to_apply=%add.28 | all-reduce | flops 3072 | bytes 24576
  134.0 100.0 %psum.22 = f32[384]{0:T(512)S(1)} all-reduce(f32[384]{0:T(512)S(1)} %convolution_reduce_fusion), channel_id=1, replica_groups=mesh['region'=8,'sub'=32] {'region','sub'}, use_global_device_ids=true, to_apply=%region_10.11 | all-reduce | flops 384 | bytes 3072 | tf_op jit(solution)/shard_map/psum | solution.py:128
  239.4 4.3 %scatter-add.44 = f32[3,16,256]{1,0,2:T(4,128)S(1)} dynamic-update-slice(f32[3,16,256]{1,0,2:T(4,128)S(1)} %scatter_fusion, f32[3,1,256]{1,0,2:T(4,128)S(1)} %slice_add_fusion, s32[]{:T(128)} %constant.334.clone.1, s32[]{:T(128)} %constant.334.clone.1, s32[]{:T(128)} %constant.334.clone.1) | dynamic-update-slice | bytes 6148 | tf_op jit(solution)/shard_map/scatter-add | solution.py:120
  244.8 2.0 fusion.17
  246.9 2.0 add_subtract_fusion.1
  249.0 4.8 %reshape.713 = f32[3,8,2,8,2,8,2]{6,5,4,3,2,1,0:T(8,128)} reshape(f32[3,16,256]{2,1,0:T(8,128)S(1)} %copy.135) | data formatting | bytes 98304 | tf_op jit(solution)/shard_map/reshape | solution.py:36
  253.8 2.2 reduce_sum.73
  259.1 2.1 bitcast_add_fusion.1
  261.2 2.1 divide_add_fusion.2
  263.3 2.1 divide_add_fusion.1
  265.3 2.2 add_subtract_fusion
  267.7 4.8 %reshape.721 = f32[3,8,2,8,2,8,2]{6,5,4,3,2,1,0:T(8,128)} reshape(f32[3,16,256]{2,1,0:T(8,128)S(1)} %copy.147) | data formatting | bytes 98304 | tf_op jit(solution)/shard_map/reshape | solution.py:36
  272.5 2.2 reduce_sum.77
  277.9 2.1 divide_add_fusion
  280.2 1.1 scatter_fusion.2
  281.4 1.1 collective-permute-start.3
  283.6 1.3 collective-permute-start.5
  285.0 2.1 collective-permute-start.4
  287.8 3.6 collective-permute-done.4
  292.1 74.3 %all-reduce.29 = (f32[]{:T(128)}, f32[]{:T(128)}) all-reduce(f32[]{:T(128)} %multiply_reduce_fusion, f32[]{:T(128)} %fusion.100), channel_id=1, replica_groups=mesh['region'=8,'sub'=32] {'region','sub'}, use_global_device_ids=true, to_apply=%region_1.0 | all-reduce | flops 2 | bytes 16 | tf_op jit(solution)/shard_map/psum | solution.py:148
  (186 shorter events, 22.8 us)
Async XLA Ops:
  0.6 234.1 %copy-start = (f32[1,96,3072]{2,1,0:T(8,128)S(1)}, f32[1,96,3072]{2,1,0:T(8,128)}, u32[]{:S(2)}) copy-start(f32[1,96,3072]{2,1,0:T(8,128)} %param.23) | copy-start | bytes 3538948
  1.5 237.1 %collective-permute-start = (f32[3,256]{1,0:T(4,128)S(1)}, f32[3,256]{1,0:T(4,128)S(1)}, u32[]{:S(2)}, u32[]{:S(2)}) collective-permute-start(f32[3,256]{1,0:T(4,128)S(1)} %bitcast.182), channel_id=1, source_target_pairs={{0,32},{32,64},{64,96},{96,128},{128,160},{160,192},{192,224},{224... | collective-permute-start | bytes 9224 | tf_op jit(solution)/shard_map/ppermute | solution.py:16
  4.1 234.8 %collective-permute-start.1 = (f32[3,256]{1,0:T(4,128)S(1)}, f32[3,256]{1,0:T(4,128)S(1)}, u32[]{:S(2)}, u32[]{:S(2)}) collective-permute-start(f32[3,256]{1,0:T(4,128)S(1)} %bitcast.181), channel_id=1, source_target_pairs={{0,4},{1,5},{2,6},{3,7},{4,8},{5,9},{6,10},{7,11},{8,12},{9,13},{1... | collective-permute-start | bytes 9224 | tf_op jit(solution)/shard_map/ppermute | solution.py:16
  11.0 228.0 %collective-permute-start.2 = (f32[3,256]{1,0:T(4,128)S(1)}, f32[3,256]{1,0:T(4,128)S(1)}, u32[]{:S(2)}, u32[]{:S(2)}) collective-permute-start(f32[3,256]{1,0:T(4,128)S(1)} %bitcast.180), channel_id=1, source_target_pairs={{0,1},{1,2},{2,3},{3,4},{4,5},{5,6},{6,7},{7,8},{8,9},{9,10},{10,1... | collective-permute-start | bytes 9224 | tf_op jit(solution)/shard_map/ppermute | solution.py:16
  15.1 1.3 copy-start.8
  15.1 1.3 copy-start.4
  15.4 2.3 copy-start.9
  15.4 118.4 %copy-start.2 = (f32[1,96,384]{2,1,0:T(8,128)S(1)}, f32[1,96,384]{2,1,0:T(8,128)}, u32[]{:S(2)}) copy-start(f32[1,96,384]{2,1,0:T(8,128)} %param.24) | copy-start | bytes 442372
  15.6 218.4 %copy-start.5 = (f32[1,3,3,256]{3,0,2,1:T(1,128)S(1)}, f32[1,3,3,256]{3,0,2,1:T(1,128)}, u32[]{:S(2)}) copy-start(f32[1,3,3,256]{3,0,2,1:T(1,128)} %param.19) | copy-start | bytes 27652
  16.0 219.7 %copy-start.1 = (f32[384,384]{1,0:T(8,128)S(1)}, f32[384,384]{1,0:T(8,128)}, u32[]{:S(2)}) copy-start(f32[384,384]{1,0:T(8,128)} %param.25) | copy-start | bytes 1769476
  234.7 2.4 copy-start.3
  280.2 88.2 %copy-start.7 = (f32[1,3,3,256]{3,0,2,1:T(1,128)S(1)}, f32[1,3,3,256]{3,0,2,1:T(1,128)}, u32[]{:S(2)}) copy-start(f32[1,3,3,256]{3,0,2,1:T(1,128)} %param.17) | copy-start | bytes 27652
  280.2 88.8 %copy-start.6 = (f32[1,16,256]{2,1,0:T(8,128)S(1)}, f32[1,16,256]{2,1,0:T(8,128)}, u32[]{:S(2)}) copy-start(f32[1,16,256]{2,1,0:T(8,128)} %param.21) | copy-start | bytes 49156
  281.4 6.0 %collective-permute-start.3 = (f32[3,256]{1,0:T(4,128)S(1)}, f32[3,256]{1,0:T(4,128)S(1)}, u32[]{:S(2)}, u32[]{:S(2)}) collective-permute-start(f32[3,256]{1,0:T(4,128)S(1)} %bitcast.183), channel_id=1, source_target_pairs={{0,224},{32,0},{64,32},{96,64},{128,96},{160,128},{192,160},{224,1... | collective-permute-start | bytes 9224 | tf_op jit(solution)/shard_map/ppermute | solution.py:16
  283.6 3.8 %collective-permute-start.5 = (f32[3,256]{1,0:T(4,128)S(1)}, f32[3,256]{1,0:T(4,128)S(1)}, u32[]{:S(2)}, u32[]{:S(2)}) collective-permute-start(f32[3,256]{1,0:T(4,128)S(1)} %reshape.734), channel_id=1, source_target_pairs={{0,31},{1,0},{2,1},{3,2},{4,3},{5,4},{6,5},{7,6},{8,7},{9,8},{10,9... | collective-permute-start | bytes 9224 | tf_op jit(solution)/shard_map/ppermute | solution.py:16
  285.0 6.4 %collective-permute-start.4 = (f32[3,256]{1,0:T(4,128)S(1)}, f32[3,256]{1,0:T(4,128)S(1)}, u32[]{:S(2)}, u32[]{:S(2)}) collective-permute-start(f32[3,256]{1,0:T(4,128)S(1)} %reshape.732), channel_id=1, source_target_pairs={{0,28},{1,29},{2,30},{3,31},{4,0},{5,1},{6,2},{7,3},{8,4},{9,5},{1... | collective-permute-start | bytes 9224 | tf_op jit(solution)/shard_map/ppermute | solution.py:16
where the time goes:
time: 371 us; the launch traced here: 370 us
  blocking collectives  289 us (78%)
  other arithmetic  29.4 us (8%)
  local copies, waits for them, and re-layouts  27.2 us (7%)
  starting transfers between devices  14.8 us (4%)
    unnamed x1, blocking collectives  115 us
    psum x1, blocking collectives, body(): total = lax.psum(share, ('region', 'sub'))  100 us
    psum x1, blocking collectives, body(): lax.psum((jnp.sum(active * jump), squares), ('region', 'sub'))  74.3 us
    ppermute x6, starting transfers between devices, shifted_2(): return lax.ppermute(x, axis, [(i, (i + by) % count) for i in range(count)])  14.8 us
    reshape x4, local copies, waits for them, and re-layouts, restrict(): array.reshape(lead + (depth // 2, 2, half, 2, half, 2))  10.7 us
    add x17, other arithmetic, relax(): field + damping * (source - operate(field, react, weight, cells)) / diagonal  7.44 us
  transfers between devices with their start and end apart: 6, of which 1 were waited for; matrix products, arithmetic and copies ran while one was open for 4% of the time, Pallas kernels for 0%

commit v1 on v0

--- a/solution.py
+++ b/solution.py
@@ -125,7 +125,7 @@
     rows = region_inverse[0]
     mapping = coarse_map[0]
     share = jnp.dot(primal, mapping, precision=highest)
-    total = lax.psum(share, ("region", "sub"))
+    total = lax.psum(lax.psum(share, "sub"), "region")
     region_part = jnp.dot(
         rows, lax.all_gather(primal, "sub", axis=0, tiled=True), precision=highest
     )

time: 371 us -> 307 us (0.83)
  blocking collectives: 289 us -> 227 us
  starting transfers between devices: 14.8 us -> 11 us
    psum x1, blocking collectives: 100 us -> 38.7 us  [body(): total = lax.psum(lax.psum(share, 'sub'), 'region')]
    ppermute x6, starting transfers between devices: 14.8 us -> 11 us  [shifted_2(): return lax.ppermute(x, axis, [(i, (i + by) % count) for i in range(count)])]
  transfers between devices with their start and end apart: 6 -> 6, of which waited for: 1 -> 3; matrix products, arithmetic and copies ran while one was open for 4% -> 4% of each run, Pallas kernels for 0% -> 0%
where the time goes in v1:
time: 307 us; the launch traced here: 306 us
  blocking collectives  227 us (74%)
  other arithmetic  29.4 us (10%)
  local copies, waits for them, and re-layouts  27.2 us (9%)
  starting transfers between devices  11 us (4%)
  waiting for transfers between devices  5.69 us (2%)
  between operations  3.48 us (1%)
    unnamed x1, blocking collectives  115 us
    psum x1, blocking collectives, body(): lax.psum((jnp.sum(active * jump), squares), ('region', 'sub'))  74 us
    psum x1, blocking collectives, body(): total = lax.psum(lax.psum(share, 'sub'), 'region')  38.7 us
    ppermute x6, starting transfers between devices, shifted_2(): return lax.ppermute(x, axis, [(i, (i + by) % count) for i in range(count)])  11 us
    reshape x4, local copies, waits for them, and re-layouts, restrict(): array.reshape(lead + (depth // 2, 2, half, 2, half, 2))  10.7 us
    add x17, other arithmetic, relax(): field + damping * (source - operate(field, react, weight, cells)) / diagonal  7.44 us
  transfers between devices with their start and end apart: 6, of which 3 were waited for; matrix products, arithmetic and copies ran while one was open for 4% of the time, Pallas kernels for 0%

profile of v1, /device:TPU:1, one launch (start us, length us, event | category | flops | bytes accessed | tf_op | source)
XLA Modules:
  0.0 306.3 jit_solution(13002154702716550348)
XLA Ops:
  1.5 2.6 collective-permute-start
  4.1 6.9 %collective-permute-start.1 = (f32[3,256]{1,0:T(4,128)S(1)}, f32[3,256]{1,0:T(4,128)S(1)}, u32[]{:S(2)}, u32[]{:S(2)}) collective-permute-start(f32[3,256]{1,0:T(4,128)S(1)} %bitcast.181), channel_id=1, source_target_pairs={{0,4},{1,5},{2,6},{3,7},{4,8},{5,9},{6,10},{7,11},{8,12},{9,13},{1... | collective-permute-start | bytes 9224 | tf_op jit(solution)/shard_map/ppermute | solution.py:16
  13.2 1.7 reshape_squeeze.17
  16.5 1.1 gather_fusion
  19.3 114.8 %all-reduce.30 = (f32[3072]{0:T(1024)S(1)}, f32[384]{0:T(512)S(1)}) all-reduce(f32[3072]{0:T(1024)S(1)} %fusion.269, f32[384]{0:T(512)S(1)} %convolution_reduce_fusion), channel_id=1, replica_groups=mesh['region'=8,'sub'=32] {'sub'}, use_global_device_ids=true, to_apply=%add.28 | all-reduce | flops 3456 | bytes 27648
  134.0 38.7 %psum.30 = f32[384]{0:T(512)S(1)} all-reduce(f32[384]{0:T(512)S(1)} %get-tuple-element.77), channel_id=1, replica_groups=mesh['region'=8,'sub'=32] {'region'}, use_global_device_ids=true, to_apply=%region_11.12 | all-reduce | flops 384 | bytes 3072 | tf_op jit(solution)/shard_map/psum | solution.py:128
  176.2 1.1 scatter_fusion
  178.1 4.3 %scatter-add.44 = f32[3,16,256]{1,0,2:T(4,128)S(1)} dynamic-update-slice(f32[3,16,256]{1,0,2:T(4,128)S(1)} %scatter_fusion, f32[3,1,256]{1,0,2:T(4,128)S(1)} %slice_add_fusion, s32[]{:T(128)} %constant.334.clone.1, s32[]{:T(128)} %constant.334.clone.1, s32[]{:T(128)} %constant.334.clone.1) | dynamic-update-slice | bytes 6148 | tf_op jit(solution)/shard_map/scatter-add | solution.py:120
  182.4 1.1 scatter_fusion.1
  183.6 2.0 fusion.17
  185.6 2.0 add_subtract_fusion.1
  187.7 4.8 %reshape.713 = f32[3,8,2,8,2,8,2]{6,5,4,3,2,1,0:T(8,128)} reshape(f32[3,16,256]{2,1,0:T(8,128)S(1)} %copy.135) | data formatting | bytes 98304 | tf_op jit(solution)/shard_map/reshape | solution.py:36
  192.6 2.2 reduce_sum.73
  197.9 2.1 bitcast_add_fusion.1
  199.9 2.1 divide_add_fusion.2
  202.0 2.1 divide_add_fusion.1
  204.1 2.2 add_subtract_fusion
  206.4 4.8 %reshape.721 = f32[3,8,2,8,2,8,2]{6,5,4,3,2,1,0:T(8,128)} reshape(f32[3,16,256]{2,1,0:T(8,128)S(1)} %copy.147) | data formatting | bytes 98304 | tf_op jit(solution)/shard_map/reshape | solution.py:36
  211.3 2.2 reduce_sum.77
  216.6 2.1 divide_add_fusion
  218.9 1.1 scatter_fusion.2
  223.2 1.2 collective-permute-done.5
  224.7 3.7 %collective-permute-done.4 = f32[3,256]{1,0:T(4,128)S(1)} collective-permute-done((f32[3,256]{1,0:T(4,128)S(1)}, f32[3,256]{1,0:T(4,128)S(1)}, u32[]{:S(2)}, u32[]{:S(2)}) %collective-permute-start.4) | collective-permute-done | bytes 3104 | tf_op jit(solution)/shard_map/ppermute | solution.py:16
  229.1 74.0 %all-reduce.29 = (f32[]{:T(128)}, f32[]{:T(128)}) all-reduce(f32[]{:T(128)} %multiply_reduce_fusion, f32[]{:T(128)} %fusion.100), channel_id=1, replica_groups=mesh['region'=8,'sub'=32] {'region','sub'}, use_global_device_ids=true, to_apply=%region_1.0 | all-reduce | flops 2 | bytes 16 | tf_op jit(solution)/shard_map/psum | solution.py:148
  (186 shorter events, 22.1 us)
Async XLA Ops:
  0.6 173.4 %copy-start = (f32[1,96,3072]{2,1,0:T(8,128)S(1)}, f32[1,96,3072]{2,1,0:T(8,128)}, u32[]{:S(2)}) copy-start(f32[1,96,3072]{2,1,0:T(8,128)} %param.23) | copy-start | bytes 3538948
  1.5 175.8 %collective-permute-start = (f32[3,256]{1,0:T(4,128)S(1)}, f32[3,256]{1,0:T(4,128)S(1)}, u32[]{:S(2)}, u32[]{:S(2)}) collective-permute-start(f32[3,256]{1,0:T(4,128)S(1)} %bitcast.182), channel_id=1, source_target_pairs={{0,32},{32,64},{64,96},{96,128},{128,160},{160,192},{192,224},{224... | collective-permute-start | bytes 9224 | tf_op jit(solution)/shard_map/ppermute | solution.py:16
  4.1 173.5 %collective-permute-start.1 = (f32[3,256]{1,0:T(4,128)S(1)}, f32[3,256]{1,0:T(4,128)S(1)}, u32[]{:S(2)}, u32[]{:S(2)}) collective-permute-start(f32[3,256]{1,0:T(4,128)S(1)} %bitcast.181), channel_id=1, source_target_pairs={{0,4},{1,5},{2,6},{3,7},{4,8},{5,9},{6,10},{7,11},{8,12},{9,13},{1... | collective-permute-start | bytes 9224 | tf_op jit(solution)/shard_map/ppermute | solution.py:16
  11.0 166.8 %collective-permute-start.2 = (f32[3,256]{1,0:T(4,128)S(1)}, f32[3,256]{1,0:T(4,128)S(1)}, u32[]{:S(2)}, u32[]{:S(2)}) collective-permute-start(f32[3,256]{1,0:T(4,128)S(1)} %bitcast.180), channel_id=1, source_target_pairs={{0,1},{1,2},{2,3},{3,4},{4,5},{5,6},{6,7},{7,8},{8,9},{9,10},{10,1... | collective-permute-start | bytes 9224 | tf_op jit(solution)/shard_map/ppermute | solution.py:16
  15.1 1.3 copy-start.8
  15.1 1.3 copy-start.4
  15.4 2.3 copy-start.9
  15.4 3.5 %copy-start.2 = (f32[1,96,384]{2,1,0:T(8,128)S(1)}, f32[1,96,384]{2,1,0:T(8,128)}, u32[]{:S(2)}) copy-start(f32[1,96,384]{2,1,0:T(8,128)} %param.24) | copy-start | bytes 442372
  15.6 157.1 %copy-start.5 = (f32[1,3,3,256]{3,0,2,1:T(1,128)S(1)}, f32[1,3,3,256]{3,0,2,1:T(1,128)}, u32[]{:S(2)}) copy-start(f32[1,3,3,256]{3,0,2,1:T(1,128)} %param.19) | copy-start | bytes 27652
  15.7 157.8 %copy-start.1 = (f32[384,384]{1,0:T(8,128)S(1)}, f32[384,384]{1,0:T(8,128)}, u32[]{:S(2)}) copy-start(f32[384,384]{1,0:T(8,128)} %param.25) | copy-start | bytes 1769476
  173.4 2.4 copy-start.3
  218.9 86.1 %copy-start.7 = (f32[1,3,3,256]{3,0,2,1:T(1,128)S(1)}, f32[1,3,3,256]{3,0,2,1:T(1,128)}, u32[]{:S(2)}) copy-start(f32[1,3,3,256]{3,0,2,1:T(1,128)} %param.17) | copy-start | bytes 27652
  218.9 86.7 %copy-start.6 = (f32[1,16,256]{2,1,0:T(8,128)S(1)}, f32[1,16,256]{2,1,0:T(8,128)}, u32[]{:S(2)}) copy-start(f32[1,16,256]{2,1,0:T(8,128)} %param.21) | copy-start | bytes 49156
  220.2 3.0 collective-permute-start.3
  221.9 2.5 collective-permute-start.5
  222.0 6.4 %collective-permute-start.4 = (f32[3,256]{1,0:T(4,128)S(1)}, f32[3,256]{1,0:T(4,128)S(1)}, u32[]{:S(2)}, u32[]{:S(2)}) collective-permute-start(f32[3,256]{1,0:T(4,128)S(1)} %reshape.732), channel_id=1, source_target_pairs={{0,28},{1,29},{2,30},{3,31},{4,0},{5,1},{6,2},{7,3},{8,4},{9,5},{1... | collective-permute-start | bytes 9224 | tf_op jit(solution)/shard_map/ppermute | solution.py:16
